TPU v7x, 32 devices: a whole 2x2x4 slice. The times are simulated.
32 devices in a mesh: fsdp: 32 (over z, y, x, core).
Axes of the slice: x: 2, y: 2, z: 4, core: 2. Of those that a mesh axis runs over, the one named last changes fastest.
Arguments:
- characters: bfloat16 [2, 8192, 768], P(None, 'fsdp'), may hold values from -6 to 6
- segment_ids: int32 [2, 8192], P(None, 'fsdp'), may hold values from 0 to 31, never falling along the last dimension, each value on 1 to 1024 neighbouring positions
- cotangent: bfloat16 [2, 2048, 768], P(None, 'fsdp'), may hold values from -6 to 6
- local_params: bfloat16 [7087104], P('fsdp'), may hold values from -3 to 3, as said below
- conv_params: bfloat16 [2361600], P('fsdp'), may hold values from -3 to 3, as said below
Outputs:
- molecules: bfloat16 [2, 2048, 768], P(None, 'fsdp')
- char_grads: float32 [2, 8192, 768], P(None, 'fsdp')
- local_grads: float32 [7087104], P('fsdp')
- conv_grads: float32 [2361600], P('fsdp')
Inputs may be any that keep to these rules, and one draw needn't show every extreme that they name: `local_params`: holds the layer's parameters flattened in the order of the first step (matrices row-major), the last 0 entries being padding that no output reads. `conv_params`: holds Wc row-major, then bc, g3, s3, the last 0 entries being padding that no output reads.
All inputs are finite; a program needn't handle non-finite values.
Results may differ from a plain program's by a relative error of at most 0.014.
Values may be sent and summed in bfloat16 or wider, within the bound.
A program may use at most 256 MiB of HBM per device.

v0:
```python
import math

import jax
import jax.numpy as jnp
from jax import lax
from jax.sharding import PartitionSpec as P

D = 768
HEADS = 12
FF = 3072
WINDOW = 128
RATE = 4
MICRO = 2
HEAD_SIZE = 64
LOCAL_COUNT = 7087104
CONV_COUNT = 2361600


EPSILON = 1e-05


def local_layout():
    return ((D, 3 * D), (D, D), (D, FF), (FF, D), (FF,)) + ((D,),) * 8


def conv_layout():
    return ((RATE * D, D), (D,), (D,), (D,))


def unpack(packed, layout):
    offset = 0
    pieces = []
    for extent in layout:
        length = math.prod(extent)
        pieces.append(packed[offset : offset + length].reshape(extent))
        offset = offset + length
    return pieces


def normalize_parts(values):
    average = jnp.mean(values, axis=-1, keepdims=True)
    centred = values - average
    spread = jnp.mean(centred * centred, axis=-1, keepdims=True)
    scaling = lax.rsqrt(spread + EPSILON)
    return (centred * scaling, scaling)


def normal_back(grad_normed, normed, scaling):
    first_mean = jnp.mean(grad_normed, axis=-1, keepdims=True)
    second_mean = jnp.mean(grad_normed * normed, axis=-1, keepdims=True)
    return scaling * (grad_normed - first_mean - normed * second_mean)


def product(left, right):
    return jnp.dot(left, right, preferred_element_type=jnp.float32)


def rows_inner(left, right):
    return lax.dot_general(
        left, right, (((0,), (0,)), ((), ())), preferred_element_type=jnp.float32
    )


def times_transpose(left, right):
    return lax.dot_general(
        left, right, (((1,), (1,)), ((), ())), preferred_element_type=jnp.float32
    )


def gelu_exact(values):
    return jax.nn.gelu(values, approximate=False)


def gelu_grad(values, upstream):
    return jax.vjp(gelu_exact, values)[1](upstream)[0]


def window_scores(projected, segments_block):
    row_count = projected.shape[0]
    windows = row_count // WINDOW
    heads_view = projected.reshape(windows, WINDOW, 3, HEADS, HEAD_SIZE)
    queries = heads_view[:, :, 0]
    keys_all = heads_view[:, :, 1]
    values = heads_view[:, :, 2]
    scores = jnp.einsum(
        "bqhe,bkhe->bhqk", queries, keys_all, preferred_element_type=jnp.float32
    ) * HEAD_SIZE ** (-0.5)
    grouped = segments_block.reshape(windows, WINDOW)
    allowed = grouped[:, None, :, None] == grouped[:, None, None, :]
    return (jnp.where(allowed, scores, -1e30), queries, keys_all, values)


def forward_pass(characters_block, segments_block, local_weights, conv_weights):
    (
        qkv_weight,
        out_weight,
        in_weight,
        down_weight,
        in_bias,
        gain_one,
        shift_one,
        query_bias,
        value_bias,
        out_bias,
        gain_two,
        shift_two,
        down_bias,
    ) = local_weights
    conv_weight, conv_bias, gain_three, shift_three = conv_weights
    row_count = characters_block.shape[0]
    inputs = characters_block.astype(jnp.float32)
    norm_one, scale_one = normalize_parts(inputs)
    normed = (norm_one * gain_one + shift_one).astype(jnp.bfloat16)
    proj_bias = jnp.concatenate([query_bias, jnp.zeros_like(query_bias), value_bias])
    projected = (product(normed, qkv_weight) + proj_bias).astype(jnp.bfloat16)
    scores, queries, keys_all, values = window_scores(projected, segments_block)
    largest = jnp.max(scores, axis=-1, keepdims=True)
    raised = jnp.exp(scores - largest)
    totals = jnp.sum(raised, axis=-1, keepdims=True)
    log_totals = largest + jnp.log(totals)
    weights = (raised / totals).astype(jnp.bfloat16)
    attended = jnp.einsum("bhqk,bkhe->bqhe", weights, values, preferred_element_type=jnp.float32)
    context = attended.reshape(row_count, D).astype(jnp.bfloat16)
    after_attention = inputs + product(context, out_weight) + out_bias
    norm_two, scale_two = normalize_parts(after_attention)
    middle = (norm_two * gain_two + shift_two).astype(jnp.bfloat16)
    pre_act = product(middle, in_weight) + in_bias
    hidden = gelu_exact(pre_act).astype(jnp.bfloat16)
    after_feed = after_attention + product(hidden, down_weight) + down_bias
    grouped_rows = after_feed.astype(jnp.bfloat16).reshape(row_count // RATE, RATE * D)
    conv_pre = product(grouped_rows, conv_weight) + conv_bias
    norm_three, scale_three = normalize_parts(gelu_exact(conv_pre))
    molecules = (norm_three * gain_three + shift_three).astype(jnp.bfloat16)
    saved_state = (
        segments_block,
        norm_one,
        scale_one,
        normed,
        projected,
        log_totals,
        context,
        norm_two,
        scale_two,
        middle,
        pre_act,
        hidden,
        grouped_rows,
        conv_pre,
        norm_three,
        scale_three,
    )
    return (molecules, saved_state)


def backward_pass(cotangent_block, saved_state, local_weights, conv_weights):
    (
        qkv_weight,
        out_weight,
        in_weight,
        down_weight,
        in_bias,
        gain_one,
        shift_one,
        query_bias,
        value_bias,
        out_bias,
        gain_two,
        shift_two,
        down_bias,
    ) = local_weights
    conv_weight, conv_bias, gain_three, shift_three = conv_weights
    (
        segments_block,
        norm_one,
        scale_one,
        normed,
        projected,
        log_totals,
        context,
        norm_two,
        scale_two,
        middle,
        pre_act,
        hidden,
        grouped_rows,
        conv_pre,
        norm_three,
        scale_three,
    ) = saved_state
    row_count = normed.shape[0]
    windows = row_count // WINDOW
    upstream = cotangent_block.astype(jnp.float32)
    grad_gain_three = jnp.sum(upstream * norm_three, axis=0)
    grad_shift_three = jnp.sum(upstream, axis=0)
    grad_activated = normal_back(upstream * gain_three, norm_three, scale_three)
    grad_conv_pre = gelu_grad(conv_pre, grad_activated).astype(jnp.bfloat16)
    grad_conv_bias = jnp.sum(grad_conv_pre.astype(jnp.float32), axis=0)
    grad_conv_weight = rows_inner(grouped_rows, grad_conv_pre)
    grad_feed = times_transpose(grad_conv_pre, conv_weight).reshape(row_count, D)
    grad_down_bias = jnp.sum(grad_feed, axis=0)
    grad_branch = grad_feed.astype(jnp.bfloat16)
    grad_down_weight = rows_inner(hidden, grad_branch)
    grad_hidden = times_transpose(grad_branch, down_weight)
    grad_pre = gelu_grad(pre_act, grad_hidden).astype(jnp.bfloat16)
    grad_in_bias = jnp.sum(grad_pre.astype(jnp.float32), axis=0)
    grad_in_weight = rows_inner(middle, grad_pre)
    grad_middle = times_transpose(grad_pre, in_weight)
    grad_gain_two = jnp.sum(grad_middle * norm_two, axis=0)
    grad_shift_two = jnp.sum(grad_middle, axis=0)
    grad_attention = grad_feed + normal_back(grad_middle * gain_two, norm_two, scale_two)
    grad_out_bias = jnp.sum(grad_attention, axis=0)
    grad_attn_out = grad_attention.astype(jnp.bfloat16)
    grad_out_weight = rows_inner(context, grad_attn_out)
    grad_context = times_transpose(grad_attn_out, out_weight).astype(jnp.bfloat16)
    grad_heads = grad_context.reshape(windows, WINDOW, HEADS, HEAD_SIZE)
    scores, queries, keys_all, values = window_scores(projected, segments_block)
    probs = jnp.exp(scores - log_totals)
    weights = probs.astype(jnp.bfloat16)
    grad_weights = jnp.einsum(
        "bqhe,bkhe->bhqk", grad_heads, values, preferred_element_type=jnp.float32
    )
    row_terms = jnp.sum(probs * grad_weights, axis=-1, keepdims=True)
    grad_scores = (probs * (grad_weights - row_terms)).astype(jnp.bfloat16)
    grad_queries = jnp.einsum(
        "bhqk,bkhe->bqhe", grad_scores, keys_all, preferred_element_type=jnp.float32
    ) * HEAD_SIZE ** (-0.5)
    grad_keys = jnp.einsum(
        "bhqk,bqhe->bkhe", grad_scores, queries, preferred_element_type=jnp.float32
    ) * HEAD_SIZE ** (-0.5)
    grad_values = jnp.einsum(
        "bhqk,bqhe->bkhe", weights, grad_heads, preferred_element_type=jnp.float32
    )
    grad_proj = (
        jnp.stack([grad_queries, grad_keys, grad_values], axis=2)
        .reshape(row_count, 3 * D)
        .astype(jnp.bfloat16)
    )
    proj_sums = jnp.sum(grad_proj.astype(jnp.float32), axis=0)
    grad_query_bias = proj_sums[:D]
    grad_value_bias = proj_sums[2 * D :]
    grad_qkv_weight = rows_inner(normed, grad_proj)
    grad_normed = times_transpose(grad_proj, qkv_weight)
    grad_gain_one = jnp.sum(grad_normed * norm_one, axis=0)
    grad_shift_one = jnp.sum(grad_normed, axis=0)
    grad_inputs = grad_attention + normal_back(grad_normed * gain_one, norm_one, scale_one)
    local_grad = jnp.concatenate(
        [
            grad_qkv_weight.reshape(-1),
            grad_out_weight.reshape(-1),
            grad_in_weight.reshape(-1),
            grad_down_weight.reshape(-1),
            grad_in_bias,
            grad_gain_one,
            grad_shift_one,
            grad_query_bias,
            grad_value_bias,
            grad_out_bias,
            grad_gain_two,
            grad_shift_two,
            grad_down_bias,
        ]
    )
    conv_grad = jnp.concatenate(
        [grad_conv_weight.reshape(-1), grad_conv_bias, grad_gain_three, grad_shift_three]
    )
    return (grad_inputs, local_grad, conv_grad)


def on_device(characters, segment_ids, cotangent, local_params, conv_params):
    devices = lax.axis_size("fsdp")
    local_shard = local_params.shape[0]
    conv_shard = conv_params.shape[0]
    local_pad = local_shard * devices - LOCAL_COUNT
    conv_pad = conv_shard * devices - CONV_COUNT
    local_total = jnp.zeros((1, local_shard), jnp.float32)
    conv_total = jnp.zeros((1, conv_shard), jnp.float32)
    molecule_list = []
    gradient_list = []
    for micro_index in range(MICRO):
        local_full, conv_full = (
            lax.all_gather(local_params, "fsdp", axis=0, tiled=True),
            lax.all_gather(conv_params, "fsdp", axis=0, tiled=True),
        )
        molecules, saved_state = forward_pass(
            characters[micro_index],
            segment_ids[micro_index],
            unpack(local_full, local_layout()),
            unpack(conv_full, conv_layout()),
        )
        local_full, conv_full = (
            lax.all_gather(local_params, "fsdp", axis=0, tiled=True),
            lax.all_gather(conv_params, "fsdp", axis=0, tiled=True),
        )
        grad_inputs, local_grad, conv_grad = backward_pass(
            cotangent[micro_index],
            saved_state,
            unpack(local_full, local_layout()),
            unpack(conv_full, conv_layout()),
        )
        local_table = jnp.concatenate([local_grad, jnp.zeros((local_pad,), jnp.float32)]).reshape(
            devices, local_shard
        )
        conv_table = jnp.concatenate([conv_grad, jnp.zeros((conv_pad,), jnp.float32)]).reshape(
            devices, conv_shard
        )
        local_part, conv_part = (
            lax.psum_scatter(local_table, "fsdp", scatter_dimension=0, tiled=True),
            lax.psum_scatter(conv_table, "fsdp", scatter_dimension=0, tiled=True),
        )
        local_total = local_total + local_part
        conv_total = conv_total + conv_part
        molecule_list.append(molecules)
        gradient_list.append(grad_inputs)
    return (
        jnp.stack(molecule_list),
        jnp.stack(gradient_list),
        local_total.reshape(-1),
        conv_total.reshape(-1),
    )


def solution(mesh):
    return jax.shard_map(
        on_device,
        mesh=mesh,
        in_specs=(
            P(None, "fsdp", None),
            P(None, "fsdp"),
            P(None, "fsdp", None),
            P("fsdp"),
            P("fsdp"),
        ),
        out_specs=(P(None, "fsdp", None), P(None, "fsdp", None), P("fsdp"), P("fsdp")),
        check_vma=False,
    )
```

profile of v0, /device:TPU:15, one launch (start us, length us, event | category | flops | bytes accessed | tf_op | source)
XLA Modules:
  0.0 1393.8 jit_solution(18245568424642961688)
XLA Ops:
  12.5 7.6 dynamic-update-slice
  28.9 304.1 %all-reduce.11.cloned.1.call-done = (bf16[7087104]{0:T(1024)(128)(2,1)}, bf16[2361600]{0:T(1024)(128)(2,1)}) async-done(((bf16[7087104]{0:T(1024)(128)(2,1)}, bf16[2361600]{0:T(1024)(128)(2,1)}), (bf16[7087104]{0:T(1024)(128)(2,1)}, bf16[2361600]{0:T(1024)(128)(2,1)})) %all-reduce.11.cloned.1.call-update) | async-done | bytes 18897424
  339.2 8.3 fusion.184
  371.0 8.4 slice.217
  382.3 9.3 slice.220
  391.7 12.3 multiply_convert_fusion
  406.8 9.2 slice.223
  432.1 19.5 %multiply_convert_fusion.1 = (bf16[256,3072]{1,0:T(8,128)(2,1)S(1)}, f32[256,3072]{1,0:T(8,128)}, f32[256,3072]{1,0:T(8,128)}) fusion(f32[3072]{0:T(1024)S(1)} %copy-done.80, bf16[768,3072]{1,0:T(8,128)(2,1)S(1)} %bitcast.313, f32[256,768]{1,0:T(8,128)S(1)} %get-tuple-element.109, f32[768]{0:T(1024)S(1)} %get-tuple-element.129, ...), kind=kOutput, calls=%fused_computation.30 | convolution fusion | flops 1260847104 | bytes 13389824 | tf_op jit(solution)/shard_map/dot_general | solution.py:55
  570.7 8.0 reshape.419
  587.0 9.4 copy.97
  596.4 10.8 reshape.422
  607.3 7.9 reshape.424
  623.6 9.4 copy.98
  633.0 10.8 reshape.427
  647.2 9.3 constant_dynamic-update-slice_fusion.20
  656.5 8.4 constant_dynamic-update-slice_fusion.18
  698.8 28.6 %add.269 = f32[7087104]{0:T(1024)} add(f32[7087104]{0:T(1024)} %constant_dynamic-update-slice_fusion, f32[7087104]{0:T(1024)} %constant_dynamic-update-slice_fusion.1) | non-fusion elementwise | flops 7087104 | bytes 85045248 | tf_op jit(solution)/shard_map/add | solution.py:310
  727.4 38.1 %reshape.435 = f32[32,221472]{1,0:T(8,128)} reshape(f32[7087104]{0:T(1024)} %add.269) | data formatting | bytes 56696832 | tf_op jit(solution)/shard_map/add | solution.py:310
  765.5 10.7 reshape.430
  776.3 10.7 reshape.432
  787.0 16.4 %maximum_add_fusion = f32[2361600]{0:T(1024)} fusion(f32[768]{0:T(1024)S(1)} %copy-done.73, f32[768]{0:T(1024)S(1)} %copy-done.64, f32[768]{0:T(1024)S(1)} %copy-done.67, f32[2359296]{0:T(1024)} %reshape.430, f32[768]{0:T(1024)S(1)} %copy-done.72, f32[768]{0:T(1024)S(1)} %copy-done.65, f32[768]{0:T(1024)S(1)} %copy-done.66, f32[2359296]{0:T(1024)} %reshape.432), kind=kLoop, calls=%fused_computation | loop fusion | flops 16531200 | bytes 28339200 | tf_op jit(solution)/shard_map/add | solution.py:311
  803.5 12.9 reshape.436
  821.3 550.8 %all-reduce.9.cloned.1.call-done = (f32[32,221472]{1,0:T(8,128)}, f32[32,73800]{1,0:T(8,128)}) async-done(((f32[32,221472]{1,0:T(8,128)}, f32[32,73800]{1,0:T(8,128)}), (f32[32,221472]{1,0:T(8,128)}, f32[32,73800]{1,0:T(8,128)})) %all-reduce.9.cloned.1.call-update) | async-done | bytes 37794832
  1372.1 11.5 dynamic-slice_reduce_fusion
  (387 shorter events, 245.8 us)
Async XLA Ops:
  7.2 325.8 %all-reduce.11.cloned.1.call-start = ((), (), s32[]{:S(2)}) async-start(), calls=%async_computation.1 | async-start | bytes 37797888
  25.9 1346.2 %all-reduce.9.cloned.1.call-start = ((), (), s32[]{:S(2)}) async-start(), calls=%async_computation | async-start | bytes 75628544
  28.0 333.0 %copy-start.68 = (f32[256]{0:T(256)}, f32[256]{0:T(256)S(1)}, u32[]{:S(2)}) copy-start(f32[256]{0:T(256)S(1)} %add_rsqrt_fusion.1) | copy-start | bytes 3076
  28.1 387.9 %copy-start.70 = (f32[256]{0:T(256)}, f32[256]{0:T(256)S(1)}, u32[]{:S(2)}) copy-start(f32[256]{0:T(256)S(1)} %add_rsqrt_fusion.3) | copy-start | bytes 3076
  348.9 30.4 %copy-start.87 = (f32[768]{0:T(1024)}, f32[768]{0:T(1024)S(1)}, u32[]{:S(2)}) copy-start(f32[768]{0:T(1024)S(1)} %get-tuple-element.127) | copy-start | bytes 9220
  391.6 13.5 copy-start.16
  391.6 13.5 copy-start.19
  391.7 13.5 copy-start.86
  431.1 21.7 %slice-start.14 = ((s8[4718592]{0:T(1024)(128)(4,1)}), s8[4194304]{0:T(1024)(128)(4,1)S(1)}, s32[]{:S(2)}) async-start(s8[4718592]{0:T(1024)(128)(4,1)} %bitcast.314), calls=%async_computation.16 | async-start | bytes 8388608
  431.7 20.0 %copy-start.23 = (f32[256,768]{1,0:T(8,128)}, f32[256,768]{1,0:T(8,128)S(1)}, u32[]{:S(2)}) copy-start(f32[256,768]{1,0:T(8,128)S(1)} %get-tuple-element.109) | copy-start | bytes 2359300
  431.7 19.9 %copy-start.77 = (f32[256]{0:T(256)}, f32[256]{0:T(256)S(1)}, u32[]{:S(2)}) copy-start(f32[256]{0:T(256)S(1)} %broadcast_multiply_fusion.10) | copy-start | bytes 3076
  432.1 19.5 %copy-start.83 = (f32[256]{0:T(256)}, f32[256]{0:T(256)S(1)}, u32[]{:S(2)}) copy-start(f32[256]{0:T(256)S(1)} %add_rsqrt_fusion.2) | copy-start | bytes 3076
  432.1 20.7 %slice-start.15 = ((s8[4718592]{0:T(1024)(128)(4,1)}), s8[524288]{0:T(1024)(128)(4,1)S(1)}, s32[]{:S(2)}) async-start(s8[4718592]{0:T(1024)(128)(4,1)} %bitcast.314), calls=%async_computation.17 | async-start | bytes 1048576
  467.6 18.0 %slice-start.2 = ((s8[4718592]{0:T(1024)(128)(4,1)}), s8[524288]{0:T(1024)(128)(4,1)S(1)}, s32[]{:S(2)}) async-start(s8[4718592]{0:T(1024)(128)(4,1)} %bitcast.298), calls=%async_computation.4 | async-start | bytes 1048576
  472.3 13.3 slice-start.3
  535.4 32.7 %copy-start.58 = (f32[256,768]{1,0:T(8,128)}, f32[256,768]{1,0:T(8,128)S(1)}, u32[]{:S(2)}) copy-start(f32[256,768]{1,0:T(8,128)S(1)} %fusion.32) | copy-start | bytes 2359300
  647.2 30.3 %slice-start.7 = ((s8[9437184]{0:T(1024)(128)(4,1)}), s8[4194304]{0:T(1024)(128)(4,1)S(1)}, s32[]{:S(2)}) async-start(s8[9437184]{0:T(1024)(128)(4,1)} %bitcast.302), calls=%async_computation.9 | async-start | bytes 8388608
  647.2 30.3 %slice-start.8 = ((s8[9437184]{0:T(1024)(128)(4,1)}), s8[4194304]{0:T(1024)(128)(4,1)S(1)}, s32[]{:S(2)}) async-start(s8[9437184]{0:T(1024)(128)(4,1)} %bitcast.302), calls=%async_computation.10 | async-start | bytes 8388608
  656.5 14.2 %copy-start.94 = (f32[768]{0:T(1024)S(1)}, f32[768]{0:T(1024)}, u32[]{:S(2)}) copy-start(f32[768]{0:T(1024)} %get-tuple-element.48) | copy-start | bytes 9220
  656.5 15.5 %copy-start.92 = (f32[768]{0:T(1024)S(1)}, f32[768]{0:T(1024)}, u32[]{:S(2)}) copy-start(f32[768]{0:T(1024)} %get-tuple-element.8) | copy-start | bytes 9220
  656.5 16.8 %copy-start.91 = (f32[768]{0:T(1024)S(1)}, f32[768]{0:T(1024)}, u32[]{:S(2)}) copy-start(f32[768]{0:T(1024)} %get-tuple-element.20) | copy-start | bytes 9220
  656.5 18.1 %copy-start.93 = (f32[768]{0:T(1024)S(1)}, f32[768]{0:T(1024)}, u32[]{:S(2)}) copy-start(f32[768]{0:T(1024)} %get-tuple-element.84) | copy-start | bytes 9220
  656.5 19.3 %copy-start.9 = (f32[589824]{0:T(1024)S(1)}, f32[589824]{0:T(1024)}, u32[]{:S(2)}) copy-start(f32[589824]{0:T(1024)} %reshape.425) | copy-start | bytes 7077892
  656.5 21.0 %slice-start.9 = ((s8[9437184]{0:T(1024)(128)(4,1)}), s8[1048576]{0:T(1024)(128)(4,1)S(1)}, s32[]{:S(2)}) async-start(s8[9437184]{0:T(1024)(128)(4,1)} %bitcast.302), calls=%async_computation.11 | async-start | bytes 2097152
  (91 other events, 435.8 us)
Sparse Core Ops, SparseCore 0:
  26.1 306.8 all-reduce.10
  816.6 555.4 all-reduce.8
where the time goes:
time: 1410 us; the launch traced here: 1390 us
  waiting for transfers between devices  855 us (61%)
  local copies, waits for them, and re-layouts  321 us (23%)
  matrix products  143 us (10%)
  other arithmetic  59.6 us (4%)
  between operations  15.5 us (1%)
    unnamed x4, waiting for transfers between devices  855 us
    unnamed x256, local copies, waits for them, and re-layouts  109 us
    dot_general x10, matrix products, product(): return jnp.dot(left, right, preferred_element_type=jnp.float32)  52.9 us
    slice x9, local copies, waits for them, and re-layouts, unpack(): pieces.append(packed[offset:offset + length].reshape(extent))  52.1 us
    dot_general x10, matrix products, rows_inner(): lax.dot_general(left, right, (((0,), (0,)), ((), ())), preferred_element_...  42.9 us
    add x1, local copies, waits for them, and re-layouts, on_device(): local_total = local_total + local_part  38.1 us
    dot_general x10, matrix products, times_transpose(): lax.dot_general(left, right, (((1,), (1,)), ((), ())), preferred_element_...  36.4 us
    add x1, other arithmetic, on_device(): local_total = local_total + local_part  28.6 us
  transfers between devices with their start and end apart: 2, of which 2 were waited for; matrix products, arithmetic and copies ran while one was open for 0% of the time, Pallas kernels for 0%

commit v1 on v0

--- a/solution.py
+++ b/solution.py
@@ -1,22 +1,609 @@
+import functools
 import math
+from types import SimpleNamespace
 
 import jax
 import jax.numpy as jnp
 from jax import lax
+from jax.experimental import pallas as pl
+from jax.experimental.pallas import tpu as pltpu
 from jax.sharding import PartitionSpec as P
 
-D = 768
-HEADS = 12
-FF = 3072
-WINDOW = 128
-RATE = 4
-MICRO = 2
-HEAD_SIZE = 64
-LOCAL_COUNT = 7087104
-CONV_COUNT = 2361600
-
-
-EPSILON = 1e-05
+MESH = pl.DeviceIdType.MESH
+F32, BF16 = jnp.float32, jnp.bfloat16
+D, FF, HEADS, WINDOW, RATE, MICRO, HEAD_SIZE = 768, 3072, 12, 128, 4, 2, 64
+LOCAL_COUNT, CONV_COUNT = 7087104, 2361600
+LANE = 128
+UNIT = 1152
+EPS = EPSILON = 1e-05
+
+
+DC = D // LANE
+FC = FF // LANE
+VB1, VG1, VS1, VBQ, VBV, VBO, VG2, VS2, VB2 = 0, 24, 30, 36, 42, 48, 54, 60, 66
+VBC, VG3, VS3 = 78, 84, 90
+QKV_ROW, O_ROW, W1_ROW, W2_ROW = 0, 18 * D, 24 * D, 48 * D
+
+def nn(a, b): return jnp.dot(a, b, preferred_element_type=F32)
+def nt(a, b): return lax.dot_general(a, b, (((1,), (1,)), ((), ())), preferred_element_type=F32)
+def tn(a, b): return lax.dot_general(a, b, (((0,), (0,)), ((), ())), preferred_element_type=F32)
+
+def loop(n, fn, unroll=1):
+    def body(i, _):
+        fn(i)
+        return 0
+    lax.fori_loop(0, n, body, 0, unroll=unroll)
+
+def at(i, size): return pl.ds(pl.multiple_of(i * size, size), size)
+
+def vec(r, row, blocks=DC):
+    return jnp.concatenate([r.vecs[row + i:row + i + 1, :] for i in range(blocks)], axis=1)
+
+def put(r, row, value):
+    for i in range(value.shape[1] // LANE):
+        r.vgrad[row + i:row + i + 1, :] = value[:, i * LANE:(i + 1) * LANE]
+
+def add_to(r, row, value):
+    for i in range(value.shape[1] // LANE):
+        r.vgrad[row + i:row + i + 1, :] += value[:, i * LANE:(i + 1) * LANE]
+
+def normal(v):
+    mean = jnp.mean(v, axis=-1, keepdims=True)
+    cen = v - mean
+    var = jnp.mean(cen * cen, axis=-1, keepdims=True)
+    s = lax.rsqrt(var + EPS)
+    return cen * s, s
+
+def normal_back(dn, nrm, s):
+    return s * (dn - jnp.mean(dn, axis=-1, keepdims=True) - nrm * jnp.mean(dn * nrm, axis=-1, keepdims=True))
+
+def colsum(v): return jnp.sum(v, axis=0, keepdims=True)
+
+def gelu_both(h):
+    cdf = 0.5 + 0.5 * lax.erf(h * (0.5 ** 0.5))
+    pdf = jnp.exp(-0.5 * h * h) * (1.0 / math.sqrt(2 * math.pi))
+    return h * cdf, cdf + h * pdf
+
+RB = 64
+def forward_norm(r):
+    g1, s1 = vec(r, VG1), vec(r, VS1)
+    def f(i):
+        nrm, _ = normal(r.x[at(i, RB), :].astype(F32))
+        r.a[at(i, RB), :] = (nrm * g1 + s1).astype(BF16)
+    loop(r.rows // RB, f)
+
+def forward_qkv(r):
+    bias = jnp.concatenate([vec(r, VBQ), jnp.zeros((1, D), F32), vec(r, VBV)], axis=1)
+    for i in range(18):
+        r.bias[i:i + 1, :] = bias[:, i * LANE:(i + 1) * LANE]
+    def f(i):
+        b = jnp.concatenate([r.bias[pl.ds(2 * i, 1), :], r.bias[pl.ds(2 * i + 1, 1), :]], axis=1)
+        r.P[:, at(i, 256)] = (nn(r.a[...], r.wqkv[:, at(i, 256)]) + b).astype(BF16)
+    loop(9, f)
+
+def halves(v):
+    lo = lax.broadcasted_iota(jnp.int32, v.shape, 1) < 64
+    w = v.astype(F32)
+    z = jnp.zeros_like(w)
+    return jnp.concatenate([jnp.where(lo, w, z), jnp.where(lo, z, w)], axis=0).astype(BF16)
+
+def pick(v):
+    lo = lax.broadcasted_iota(jnp.int32, (WINDOW, LANE), 1) < 64
+    return jnp.where(lo, v[:WINDOW], v[WINDOW:])
+
+def heads_of(r, i):
+    w = i // DC
+    hp = lax.rem(i, DC)
+    rows = at(w, WINDOW)
+    return w, rows, at(hp, LANE), at(hp + DC, LANE), at(hp + 2 * DC, LANE)
+
+def forward_attention(r):
+    def f(i):
+        w, rows, cq, ck, cv = heads_of(r, i)
+        q2 = halves(r.P[rows, cq])
+        s = nt(q2, r.P[rows, ck]) * 0.125
+        same = r.segc[rows, :] == r.segr[pl.ds(w, 1), :]
+        same2 = jnp.concatenate([same.astype(F32)] * 2, axis=0) > 0.5
+        s = jnp.where(same2, s, -1e30)
+        e = jnp.exp(s - jnp.max(s, axis=-1, keepdims=True))
+        p = (e / jnp.sum(e, axis=-1, keepdims=True)).astype(BF16)
+        r.p[i] = p
+        r.ctx[rows, cq] = pick(nn(p, r.P[rows, cv])).astype(BF16)
+    loop(r.rows // WINDOW * DC, f)
+
+def forward_out(r):
+    bo = vec(r, VBO)
+    for i in range(3):
+        c = slice(i * 256, (i + 1) * 256)
+        r.y1[:, c] = r.x[:, c].astype(F32) + nn(r.ctx[...], r.wo[:, c]) + bo[:, c]
+    g2, s2 = vec(r, VG2), vec(r, VS2)
+    def f(i):
+        nrm, _ = normal(r.y1[at(i, RB), :])
+        r.c[at(i, RB), :] = (nrm * g2 + s2).astype(BF16)
+    loop(r.rows // RB, f)
+
+def forward_up(r):
+    def f(i):
+        b = jnp.concatenate([r.vecs[pl.ds(VB1 + 2 * i, 1), :], r.vecs[pl.ds(VB1 + 2 * i + 1, 1), :]], axis=1)
+        h = nn(r.c[...], r.w1[:, at(i, 256)]) + b
+        hid, slope = gelu_both(h)
+        r.hid[:, at(i, 256)] = hid.astype(BF16)
+        r.slope[:, at(i, 256)] = slope.astype(BF16)
+    loop(12, f)
+
+def forward_down(r):
+    b2 = vec(r, VB2)
+    for i in range(3):
+        c = slice(i * 256, (i + 1) * 256)
+        v = r.y1[:, c] + nn(r.hid[...], r.w2[:, c]) + b2[:, c]
+        r.ys[2 * i] = v[:, :LANE]
+        r.ys[2 * i + 1] = v[:, LANE:]
+    for j in range(RATE):
+        for c in range(DC):
+            r.u[j, :, c * LANE:(c + 1) * LANE] = r.ys[c, pl.ds(j, r.mols, stride=RATE), :].astype(BF16)
+
+def forward_conv(r):
+    z = vec(r, VBC)
+    for j in range(RATE):
+        z = z + nn(r.u[j], r.wc[j * D:(j + 1) * D, :])
+    w, slope = gelu_both(z)
+    nrm, s = normal(w)
+    r.mol[...] = (nrm * vec(r, VG3) + vec(r, VS3)).astype(BF16)
+    t = r.cot[...].astype(F32)
+    put(r, VG3, colsum(t * nrm))
+    put(r, VS3, colsum(t))
+    dw = normal_back(t * vec(r, VG3), nrm, s)
+    dz = (dw * slope).astype(BF16)
+    r.dz[...] = dz
+    put(r, VBC, colsum(dz.astype(F32)))
+
+def emit_flat(r, dst, row0, tile):
+    k, m = tile.shape[0], tile.shape[1] // LANE
+    for c in range(m):
+        r.scr[pl.ds(c, k, stride=m), :] = tile[:, c * LANE:(c + 1) * LANE]
+    dst[pl.ds(pl.multiple_of(row0, 16), k * m), :] = r.scr[0:k * m, :].astype(BF16)
+
+def grad_conv_weight(r):
+    for j in range(RATE):
+        def f(i):
+            emit_flat(r, r.gc, (j * D + i * 256) * DC, tn(r.u[j, :, at(i, 256)], r.dz[...]))
+        loop(3, f)
+
+def back_conv(r):
+    for j in range(RATE):
+        v = nt(r.dz[...], r.wc[j * D:(j + 1) * D, :])
+        for c in range(DC):
+            r.ys[c, pl.ds(j, r.mols, stride=RATE), :] = v[:, c * LANE:(c + 1) * LANE]
+    for c in range(DC):
+        v = r.ys[c]
+        r.df[:, c * LANE:(c + 1) * LANE] = v.astype(BF16)
+        put(r, VB2 + c, colsum(v))
+
+def grad_down_weight(r):
+    loop(12, lambda i: emit_flat(r, r.gl, W2_ROW + i * 256 * DC, tn(r.hid[:, at(i, 256)], r.df[...])))
+
+def back_down(r):
+    def f(i):
+        dh = (nt(r.df[...], r.w2[at(i, 256), :]) * r.slope[:, at(i, 256)].astype(F32)).astype(BF16)
+        r.slope[:, at(i, 256)] = dh
+        s = colsum(dh.astype(F32))
+        r.vgrad[pl.ds(VB1 + 2 * i, 1), :] = s[:, :LANE]
+        r.vgrad[pl.ds(VB1 + 2 * i + 1, 1), :] = s[:, LANE:]
+    loop(12, f)
+
+def grad_up_weight(r):
+    loop(6, lambda i: emit_flat(r, r.gl, W1_ROW + i * 128 * FC, tn(r.c[:, at(i, 128)], r.slope[...])))
+
+def back_up(r):
+    for i in range(3):
+        r.dc[:, i * 256:(i + 1) * 256] = nt(r.slope[...], r.w1[i * 256:(i + 1) * 256, :])
+    g2 = vec(r, VG2)
+    zero = jnp.zeros((1, D), F32)
+    put(r, VG2, zero); put(r, VS2, zero); put(r, VBO, zero)
+    def f(i):
+        rows = at(i, RB)
+        dc = r.dc[rows, :]
+        nrm, s = normal(r.y1[rows, :])
+        add_to(r, VG2, colsum(dc * nrm))
+        add_to(r, VS2, colsum(dc))
+        dy2 = jnp.concatenate([r.ys[c, rows, :] for c in range(DC)], axis=1)
+        dy1 = dy2 + normal_back(dc * g2, nrm, s)
+        r.dc[rows, :] = dy1
+        add_to(r, VBO, colsum(dy1))
+        r.df[rows, :] = dy1.astype(BF16)
+    loop(r.rows // RB, f)
+
+def grad_out_weight(r):
+    loop(3, lambda i: emit_flat(r, r.gl, O_ROW + i * 256 * DC, tn(r.ctx[:, at(i, 256)], r.df[...])))
+
+def back_out(r):
+    for i in range(3):
+        r.c[:, i * 256:(i + 1) * 256] = nt(r.df[...], r.wo[i * 256:(i + 1) * 256, :]).astype(BF16)
+
+def back_attention(r):
+    def f(i):
+        w, rows, cq, ck, cv = heads_of(r, i)
+        do2 = halves(r.c[rows, cq])
+        q2 = halves(r.P[rows, cq])
+        k = r.P[rows, ck]
+        pb = r.p[i]
+        p = pb.astype(F32)
+        dp = nt(do2, r.P[rows, cv])
+        ds = (p * (dp - jnp.sum(p * dp, axis=-1, keepdims=True))).astype(BF16)
+        dq = pick(nn(ds, k)) * 0.125
+        dk = tn(ds, q2) * 0.125
+        dv = tn(pb, do2)
+        r.P[rows, cq] = dq.astype(BF16)
+        r.P[rows, ck] = dk.astype(BF16)
+        r.P[rows, cv] = dv.astype(BF16)
+    loop(r.rows // WINDOW * DC, f)
+
+def grad_qkv_weight(r):
+    for c in range(DC):
+        r.vgrad[VBQ + c:VBQ + c + 1, :] = colsum(r.P[:, c * LANE:(c + 1) * LANE].astype(F32))
+        r.vgrad[VBV + c:VBV + c + 1, :] = colsum(r.P[:, 2 * D + c * LANE:2 * D + (c + 1) * LANE].astype(F32))
+    loop(6, lambda i: emit_flat(r, r.gl, QKV_ROW + i * 128 * 18, tn(r.a[:, at(i, 128)], r.P[...])))
+
+def back_qkv(r):
+    for i in range(3):
+        r.y1[:, i * 256:(i + 1) * 256] = nt(r.P[...], r.wqkv[i * 256:(i + 1) * 256, :])
+    g1 = vec(r, VG1)
+    zero = jnp.zeros((1, D), F32)
+    put(r, VG1, zero); put(r, VS1, zero)
+    def f(i):
+        rows = at(i, RB)
+        da = r.y1[rows, :]
+        nrm, s = normal(r.x[rows, :].astype(F32))
+        add_to(r, VG1, colsum(da * nrm))
+        add_to(r, VS1, colsum(da))
+        r.dc[rows, :] = r.dc[rows, :] + normal_back(da * g1, nrm, s)
+    loop(r.rows // RB, f)
+
+def state_shapes(rows):
+    mols = rows // RATE
+    V = pltpu.VMEM
+    return dict(
+        a=V((rows, D), BF16), P=V((rows, 3 * D), BF16), p=V((rows // WINDOW * DC, 2 * WINDOW, LANE), BF16),
+        ctx=V((rows, D), BF16), y1=V((rows, D), F32), c=V((rows, D), BF16), slope=V((rows, FF), BF16), hid=V((rows, FF), BF16),
+        ys=V((DC, rows, LANE), F32), u=V((RATE, mols, D), BF16), dz=V((mols, D), BF16), df=V((rows, D), BF16), dc=V((rows, D), F32),
+        scr=V((128 * FC, LANE), F32), bias=V((24, LANE), F32), vecs=V((96, LANE), F32))
+
+
+class Geo:
+    def __init__(self, n, local_shard, conv_shard):
+        self.n = n
+        self.Z = n // 8
+        self.RL = (12 * D * D) // LANE // n
+        self.RC = (4 * D * D) // LANE // n
+        self.dl = local_shard - self.RL * LANE
+        self.dc = conv_shard - self.RC * LANE
+        self.HL = -(-(self.dl * n) // (8 * LANE)) * 8
+        self.HC = -(-(self.dc * n) // (8 * LANE)) * 8
+        self.XL = -(-local_shard // (8 * LANE)) * 8
+        self.XC = -(-conv_shard // (8 * LANE)) * 8
+
+def where_am_i():
+    me = lax.axis_index("fsdp")
+    core = lax.rem(me, 2)
+    bx = lax.rem(me // 2, 2)
+    by = lax.rem(me // 4, 2)
+    z = me // 8
+    sib = me + 1 - 2 * core
+    xn = me + 2 - 4 * bx
+    yn = me + 4 - 8 * by
+    first = xn + core * (yn - xn)
+    second = yn + core * (xn - yn)
+    return me, core, z, sib, first, second
+
+def realign(out_ref, out_base, lo, hi, x_ref, shift):
+    q = shift // LANE
+    r = lax.rem(shift, LANE)
+    turn = lax.rem(LANE - r, LANE)
+    lane = lax.broadcasted_iota(jnp.int32, (16, LANE), 1)
+    keep = lane < (LANE - r)
+    def body(i, _):
+        low = x_ref[pl.ds(q + i * 16, 16), :]
+        high = x_ref[pl.ds(q + i * 16 + 1, 16), :]
+        val = jnp.where(keep, pltpu.roll(low, turn, 1), pltpu.roll(high, turn, 1))
+        out_ref[pl.ds(pl.multiple_of(out_base + i * 16, 16), 16), :] = val.astype(out_ref.dtype)
+        return 0
+    lax.fori_loop(lo // 16, hi // 16, body, 0, unroll=2 if (hi - lo) % 32 == 0 else 1)
+
+def widen(dst_ref, dst_base, src_ref, rows):
+    step = 248 if rows % 248 == 0 else 8
+    for i in range(rows // step):
+        dst_ref[dst_base + i * step:dst_base + (i + 1) * step, :] = src_ref[i * step:(i + 1) * step, :].astype(F32)
+
+def convert_unit(src_ref, base, w_ref, krow, cols, scr):
+    groups = UNIT // (16 * cols)
+    def body(g, _):
+        scr[0:16 * cols, :] = src_ref[pl.ds(pl.multiple_of(base + g * 16 * cols, 16), 16 * cols), :].astype(F32)
+        for cc in range(cols):
+            v = scr[pl.ds(cc, 16, stride=cols), :]
+            w_ref[pl.ds(pl.multiple_of(krow + g * 16, 16), 16), cc * LANE:(cc + 1) * LANE] = v.astype(BF16)
+        return 0
+    lax.fori_loop(0, groups, body, 0)
+
+
+def start_gather(g):
+    n, Z, geo, me, z = g.n, g.Z, g.geo, g.me, g.z
+    RL, RC = geo.RL, geo.RC
+    nxt = lax.rem(me + 1, n)
+    bar = pltpu.get_barrier_semaphore()
+    far = lax.rem(me + n + 2 * g.core - 1, n)
+    for dev in (g.sib, g.first, g.second, far):
+        pl.semaphore_signal(bar, inc=1, device_id=(dev,), device_id_type=MESH)
+    @pl.when(z > 0)
+    def _(): pl.semaphore_signal(bar, inc=1, device_id=(me - 8,), device_id_type=MESH)
+    @pl.when(z < Z - 1)
+    def _(): pl.semaphore_signal(bar, inc=1, device_id=(me + 8,), device_id_type=MESH)
+    widen(g.xlf, geo.HL, g.xl, geo.XL)
+    widen(g.xcf, geo.HC, g.xc, geo.XC)
+    HA, HB = 80, 32
+    lshift, cshift = geo.HL * LANE - geo.dl * me, geo.HC * LANE - geo.dc * me
+    realign(g.gl, me * RL, HA, RL, g.xlf, lshift)
+    realign(g.gc, me * RC, HB, RC, g.xcf, cshift)
+    pl.semaphore_wait(bar, 4 + jnp.where(z > 0, 1, 0) + jnp.where(z < Z - 1, 1, 0))
+    halo = pltpu.make_async_remote_copy(src_ref=g.hb, dst_ref=g.hr, send_sem=g.hsem.at[0], recv_sem=g.hsem.at[1], device_id=(nxt,), device_id_type=MESH)
+    halo.start()
+    halo.wait()
+    g.xlf[0:geo.HL, :] = g.hr[0:geo.HL, :].astype(F32)
+    g.xcf[0:geo.HC, :] = g.hr[geo.HL:geo.HL + geo.HC, :].astype(F32)
+    realign(g.gl, me * RL, 0, HA, g.xlf, lshift)
+    realign(g.gc, me * RC, 0, HB, g.xcf, cshift)
+    @pl.when(me == n - 1)
+    def _():
+        g.tail[...] = g.hb[...]
+
+
+def gather_weights(g):
+    n, Z, geo, me, z = g.n, g.Z, g.geo, g.me, g.z
+    RL, RC = geo.RL, geo.RC
+    sib, first, second, last = g.sib, g.first, g.second, n - 1
+    def pieces(src):
+        return ((0, g.gl.at[pl.ds(pl.multiple_of(src * RL, 16), RL)]), (1, g.gc.at[pl.ds(pl.multiple_of(src * RC, 16), RC)]))
+    def copies(src, dev, slot):
+        return [pltpu.make_async_remote_copy(src_ref=ref, dst_ref=ref, send_sem=g.ssem.at[k, slot], recv_sem=g.rsem.at[k, src], device_id=(dev,), device_id_type=MESH) for k, ref in pieces(src)]
+    def tail_copy(dev, slot):
+        return pltpu.make_async_remote_copy(src_ref=g.tail, dst_ref=g.tail, send_sem=g.tsem.at[slot], recv_sem=g.tsem.at[5], device_id=(dev,), device_id_type=MESH)
+    UP, DN, FI, SE, SI = 0, Z, 2 * Z, 3 * Z, 5 * Z
+    def send(src, dev, slot, tslot):
+        for cp in copies(src, dev, slot): cp.start()
+        @pl.when(src == last)
+        def _(): tail_copy(dev, tslot).start()
+    def await_recv(src):
+        for cp in copies(src, sib, 0): cp.wait_recv()
+        @pl.when(src == last)
+        def _(): tail_copy(sib, 0).wait_recv()
+    def drain(src, dev, slot, tslot):
+        for cp in copies(src, dev, slot): cp.wait_send()
+        @pl.when(src == last)
+        def _(): tail_copy(dev, tslot).wait_send()
+    def valid(dz): return jnp.logical_and(z + dz >= 0, z + dz < Z)
+    def src_of(dz, f, s): return me + 8 * dz + f * (first - me) + s * (second - me)
+    def column(dz, act):
+        src = src_of(dz, 0, 0)
+        zi = z + dz
+        if dz >= 0:
+            @pl.when(z > 0)
+            def _(): act(src, me - 8, DN + zi, 0)
+        if dz <= 0:
+            @pl.when(z < Z - 1)
+            def _(): act(src, me + 8, UP + zi, 1)
+        act(src, first, FI + zi, 2)
+        act(src, second, SE + zi, 3)
+        act(src, sib, SI + zi, 4)
+    def firsts(dz, act):
+        src = src_of(dz, 1, 0)
+        act(src, second, SE + Z + z + dz, 3)
+        act(src, sib, SI + Z + z + dz, 4)
+    def seconds(dz, f, act):
+        act(src_of(dz, f, 1), sib, SI + (2 + f) * Z + z + dz, 4)
+    def convert(dz):
+        for f in (0, 1):
+            for s in (0, 1):
+                src = src_of(dz, f, s)
+                await_recv(src + sib - me)
+                chip = src // 2
+                for i in range(2 * RL // UNIT):
+                    t = chip * (2 * RL // UNIT) + i
+                    base = t * UNIT
+                    @pl.when(t < 12)
+                    def _(): convert_unit(g.gl, base, g.wqkv, t * 64, 18, g.scr)
+                    @pl.when(jnp.logical_and(t >= 12, t < 16))
+                    def _(): convert_unit(g.gl, base, g.wo, (t - 12) * 192, 6, g.scr)
+                    @pl.when(jnp.logical_and(t >= 16, t < 32))
+                    def _(): convert_unit(g.gl, base, g.w1, (t - 16) * 48, 24, g.scr)
+                    @pl.when(t >= 32)
+                    def _(): convert_unit(g.gl, base, g.w2, (t - 32) * 192, 6, g.scr)
+                for i in range(2 * RC // UNIT):
+                    t = chip * (2 * RC // UNIT) + i
+                    convert_unit(g.gc, t * UNIT, g.wc, t * 192, 6, g.scr)
+    def level(k): return [0] if k == 0 else ([k, -k] if k < Z else [])
+    def guarded(k, fn):
+        for dz in level(k):
+            @pl.when(valid(dz))
+            def _(): fn(dz)
+    def e1(dz):
+        if dz != 0: await_recv(src_of(dz, 0, 0))
+        column(dz, send)
+    def e2(dz):
+        await_recv(src_of(dz, 1, 0))
+        firsts(dz, send)
+        await_recv(src_of(dz, 0, 1))
+        seconds(dz, 0, send)
+    def e4(dz):
+        await_recv(src_of(dz, 1, 1))
+        seconds(dz, 1, send)
+        convert(dz)
+    guarded(0, e1)
+    for k in range(Z):
+        guarded(k + 1, e1)
+        guarded(k, e2)
+        if k: guarded(k - 1, e4)
+    guarded(Z - 1, e4)
+    def finish(dz):
+        column(dz, drain)
+        firsts(dz, drain)
+        seconds(dz, 0, drain)
+        seconds(dz, 1, drain)
+    for k in range(Z): guarded(k, finish)
+
+
+PART = 576
+
+
+def scatter_gradients(g):
+    n, Z, geo, me, z = g.n, g.Z, g.geo, g.me, g.z
+    sib, first, second, last = g.sib, g.first, g.second, n - 1
+    own = (g.gl, g.gc)
+    size = (geo.RL, geo.RC)
+    def target(zt, f, s): return me + 8 * (zt - z) + f * (first - me) + s * (second - me)
+    def rows(k, t): return pl.ds(pl.multiple_of(t * size[k], 16), size[k])
+    def to_sib(k, t):
+        c = t // 2
+        return pltpu.make_async_remote_copy(src_ref=own[k].at[rows(k, t)], dst_ref=g.from_sib[k].at[rows(k, c)], send_sem=g.s_sib.at[k, c], recv_sem=g.r_sib.at[k, c], device_id=(sib,), device_id_type=MESH)
+    def to_second(k, zt, f):
+        t = target(zt, f, 1)
+        c = 2 * zt + f
+        return pltpu.make_async_remote_copy(src_ref=own[k].at[rows(k, t)], dst_ref=g.from_second[k].at[rows(k, c)], send_sem=g.s_second.at[k, c], recv_sem=g.r_second.at[k, c], device_id=(second,), device_id_type=MESH)
+    def to_first(k, zt):
+        t = target(zt, 1, 0)
+        return pltpu.make_async_remote_copy(src_ref=own[k].at[rows(k, t)], dst_ref=g.from_first[k].at[rows(k, zt)], send_sem=g.s_first.at[k, zt], recv_sem=g.r_first.at[k, zt], device_id=(first,), device_id_type=MESH)
+    def to_line(k, zt, up):
+        t = target(zt, 0, 0)
+        land, r = (g.from_below, g.r_below) if up else (g.from_above, g.r_above)
+        return pltpu.make_async_remote_copy(src_ref=own[k].at[rows(k, t)], dst_ref=land[k].at[rows(k, zt)], send_sem=g.s_line.at[k, zt], recv_sem=r.at[k, zt], device_id=(me + 8 if up else me - 8,), device_id_type=MESH)
+    def add_in(k, t, sources, out, out_base):
+        parts = size[k] // PART
+        def fetch(p, slot, i, go):
+            ref, c, there = sources[i]
+            cp = pltpu.make_async_copy(ref.at[pl.ds(pl.multiple_of(c * size[k] + p * PART, 16), PART)], g.tmp.at[slot, i], g.fsem.at[slot, i])
+            if there is None: go(cp)
+            else:
+                @pl.when(there)
+                def _(): go(cp)
+        for i in range(len(sources)): fetch(0, 0, i, lambda cp: cp.start())
+        for p in range(parts):
+            slot = p % 2
+            if p + 1 < parts:
+                for i in range(len(sources)): fetch(p + 1, 1 - slot, i, lambda cp: cp.start())
+            for i in range(len(sources)): fetch(p, slot, i, lambda cp: cp.wait())
+            def body(b, _):
+                at_ = pl.ds(pl.multiple_of(b * 16, 16), 16)
+                acc = own[k][pl.ds(pl.multiple_of(t * size[k] + p * PART + b * 16, 16), 16), :].astype(F32)
+                for i, (_r, _c, there) in enumerate(sources):
+                    v = g.tmp[slot, i, at_, :].astype(F32)
+                    acc = acc + (v if there is None else jnp.where(there, v, 0.0))
+                out[pl.ds(pl.multiple_of(out_base + p * PART + b * 16, 16), 16), :] = acc.astype(out.dtype)
+                return 0
+            lax.fori_loop(0, PART // 16, body, 0, unroll=4)
+    def p0(k, zt):
+        for f in (0, 1):
+            for s in (0, 1):
+                to_sib(k, target(zt, f, s) + sib - me).start()
+    def p1(k, zt):
+        for f in (0, 1):
+            t = target(zt, f, 1)
+            to_sib(k, t).wait_recv()
+            add_in(k, t, [(g.from_sib[k], t // 2, None)], own[k], t * size[k])
+            to_second(k, zt, f).start()
+    def p2(k, zt):
+        t = target(zt, 1, 0)
+        to_sib(k, t).wait_recv()
+        to_second(k, zt, 1).wait_recv()
+        add_in(k, t, [(g.from_sib[k], t // 2, None), (g.from_second[k], 2 * zt + 1, None)], own[k], t * size[k])
+        to_first(k, zt).start()
+    def p3(k, zt):
+        t = target(zt, 0, 0)
+        to_sib(k, t).wait_recv()
+        to_second(k, zt, 0).wait_recv()
+        to_first(k, zt).wait_recv()
+        above = jnp.logical_and(z >= zt, z < Z - 1)
+        below = jnp.logical_and(z <= zt, z > 0)
+        @pl.when(above)
+        def _(): to_line(k, zt, False).wait_recv()
+        @pl.when(below)
+        def _(): to_line(k, zt, True).wait_recv()
+        srcs = [(g.from_sib[k], t // 2, None), (g.from_second[k], 2 * zt, None), (g.from_first[k], zt, None), (g.from_above[k], zt, above), (g.from_below[k], zt, below)]
+        @pl.when(z == zt)
+        def _(): add_in(k, t, srcs, (g.xlf, g.xcf)[k], 0)
+        @pl.when(z != zt)
+        def _(): add_in(k, t, srcs, own[k], t * size[k])
+        @pl.when(z > zt)
+        def _(): to_line(k, zt, False).start()
+        @pl.when(z < zt)
+        def _(): to_line(k, zt, True).start()
+    def finish(k, zt):
+        for f in (0, 1):
+            for s in (0, 1):
+                to_sib(k, target(zt, f, s) + sib - me).wait_send()
+            to_second(k, zt, f).wait_send()
+        to_first(k, zt).wait_send()
+        @pl.when(z > zt)
+        def _(): to_line(k, zt, False).wait_send()
+        @pl.when(z < zt)
+        def _(): to_line(k, zt, True).wait_send()
+    steps = [(1, zt) for zt in reversed(range(Z))] + [(0, zt) for zt in reversed(range(Z))]
+    for i in range(len(steps) + 2):
+        if i < len(steps):
+            p0(*steps[i])
+            p1(*steps[i])
+        if 1 <= i <= len(steps): p2(*steps[i - 1])
+        if i >= 2: p3(*steps[i - 2])
+    for st in steps: finish(*st)
+
+
+def reduce_vectors(g):
+    Z, me, z = g.Z, g.me, g.z
+    core = lax.rem(me, 2)
+    bx, by = lax.rem(me // 2, 2), lax.rem(me // 4, 2)
+    def cp(slot, dev):
+        return pltpu.make_async_remote_copy(src_ref=g.vgrad, dst_ref=g.vland.at[slot], send_sem=g.vsem.at[0], recv_sem=g.vsem.at[1 + slot], device_id=(dev,), device_id_type=MESH)
+    def take(slot):
+        cp(slot, g.sib).wait_recv()
+        g.vgrad[...] = g.vgrad[...] + g.vland[slot]
+    def give(slot, dev):
+        c = cp(slot, dev)
+        c.start()
+        c.wait_send()
+    on = core == 1
+    @pl.when(jnp.logical_not(on))
+    def _(): give(0, g.sib)
+    @pl.when(on)
+    def _():
+        take(0)
+        @pl.when(bx == 0)
+        def _(): give(1, g.second)
+        @pl.when(bx == 1)
+        def _():
+            take(1)
+            @pl.when(by == 0)
+            def _(): give(2, g.first)
+            @pl.when(by == 1)
+            def _():
+                take(2)
+                @pl.when(z > 0)
+                def _(): take(3)
+                @pl.when(z < Z - 1)
+                def _(): give(3, me + 8)
+
+
+def place_gradients(g):
+    n, geo, me = g.n, g.geo, g.me
+    prv = lax.rem(me + n - 1, n)
+    HL, HC = geo.HL, geo.HC
+    g.fs[0:HL, :] = g.xlf[0:HL, :]
+    g.fs[HL:HL + HC, :] = g.xcf[0:HC, :]
+    cp = pltpu.make_async_remote_copy(src_ref=g.fs, dst_ref=g.fr, send_sem=g.hsem.at[2], recv_sem=g.hsem.at[3], device_id=(prv,), device_id_type=MESH)
+    cp.start()
+    cp.wait()
+    edge = me == n - 1
+    g.xlf[geo.RL:geo.RL + HL, :] = jnp.where(edge, g.vgrad[0:HL, :], g.fr[0:HL, :])
+    skip = VBC - HL
+    g.xcf[geo.RC:geo.RC + HC - skip, :] = jnp.where(edge, g.vgrad[VBC:HL + HC, :], g.fr[HL:HL + HC - skip, :])
+    realign(g.outl, 0, 0, geo.XL // 16 * 16 + 16, g.xlf, geo.dl * me)
+    realign(g.outc, 0, 0, geo.XC // 16 * 16 + 16, g.xcf, geo.dc * me)
 
 
 def local_layout():
@@ -266,7 +853,7 @@
     return (grad_inputs, local_grad, conv_grad)
 
 
-def on_device(characters, segment_ids, cotangent, local_params, conv_params):
+def plain_device(characters, segment_ids, cotangent, local_params, conv_params):
     devices = lax.axis_size("fsdp")
     local_shard = local_params.shape[0]
     conv_shard = conv_params.shape[0]
@@ -319,17 +906,86 @@
     )
 
 
+def fused_kernel(geo, rows, in_names, out_names, scratch_names, *refs):
+    n_in, n_out = len(in_names), len(out_names)
+    every = dict(zip(list(in_names) + list(out_names) + list(scratch_names), refs))
+    me, core, z, sib, first, second = where_am_i()
+    g = SimpleNamespace(n=geo.n, Z=geo.Z, geo=geo, me=me, core=core, z=z, sib=sib, first=first, second=second, rows=rows, mols=rows // RATE, **every)
+    for base in ("from_sib", "from_second", "from_first", "from_above", "from_below"):
+        setattr(g, base, (every[base + "_l"], every[base + "_c"]))
+    start_gather(g)
+    gather_weights(g)
+    g.vecs[...] = g.tail[...].astype(F32)
+    g.vgrad[...] = jnp.zeros_like(g.vgrad)
+    for f in (forward_norm, forward_qkv, forward_attention, forward_out, forward_up, forward_down, forward_conv, grad_conv_weight, back_conv,
+              grad_down_weight, back_down, grad_up_weight, back_up, grad_out_weight, back_out, back_attention, grad_qkv_weight, back_qkv):
+        f(g)
+    cgc = pltpu.make_async_copy(g.dc, g.cg, g.osem.at[0])
+    cgc.start()
+    scatter_gradients(g)
+    reduce_vectors(g)
+    place_gradients(g)
+    cgc.wait()
+
+
+def fused(n, characters, segment_ids, cotangent, local_params, conv_params):
+    geo = Geo(n, local_params.shape[0], conv_params.shape[0])
+    micro, span, _ = characters.shape
+    rows = micro * span
+    x = characters.reshape(rows, D)
+    cot = cotangent.reshape(rows // RATE, D)
+    segc = segment_ids.reshape(rows, 1)
+    segr = segment_ids.reshape(rows // WINDOW, WINDOW)
+    xl = jnp.pad(local_params, (0, geo.XL * LANE - local_params.shape[0])).reshape(geo.XL, LANE)
+    xc = jnp.pad(conv_params, (0, geo.XC * LANE - conv_params.shape[0])).reshape(geo.XC, LANE)
+    hb = jnp.concatenate([local_params[-geo.HL * LANE:], conv_params[-geo.HC * LANE:]]).reshape(geo.HL + geo.HC, LANE)
+    V = pl.BlockSpec(memory_space=pltpu.VMEM)
+    A = pl.BlockSpec(memory_space=pl.ANY)
+    S = jax.ShapeDtypeStruct
+    Z, H = geo.Z, geo.HL + geo.HC
+    ins = dict(x=x, segc=segc, segr=segr, cot=cot, xl=xl, xc=xc, hb=hb)
+    outs = dict(mol=(V, S((rows // RATE, D), BF16)), cg=(A, S((rows, D), F32)), outl=(V, S((geo.XL // 16 * 16 + 16, LANE), F32)), outc=(V, S((geo.XC // 16 * 16 + 16, LANE), F32)))
+    for name, count in (("from_sib", n // 2), ("from_second", 2 * Z), ("from_first", Z), ("from_above", Z), ("from_below", Z)):
+        outs[name + "_l"] = (A, S((count * geo.RL, LANE), BF16))
+        outs[name + "_c"] = (A, S((count * geo.RC, LANE), BF16))
+    W = pltpu.VMEM
+    DMA = pltpu.SemaphoreType.DMA
+    sc = state_shapes(rows)
+    sc.update(wqkv=W((D, 3 * D), BF16), wo=W((D, D), BF16), w1=W((D, FF), BF16), w2=W((FF, D), BF16), wc=W((FF, D), BF16))
+    sc.update(gl=W((n * geo.RL, LANE), BF16), gc=W((n * geo.RC, LANE), BF16), hr=W((H, LANE), BF16), tail=W((H, LANE), BF16),
+              xlf=W((geo.HL + geo.XL + 32, LANE), F32), xcf=W((geo.HC + geo.XC + 32, LANE), F32), vgrad=W((H, LANE), F32), vland=W((4, H, LANE), F32),
+              fs=W((H, LANE), F32), fr=W((H, LANE), F32), tmp=W((2, 5, PART, LANE), BF16))
+    sc.update(rsem=DMA((2, n)), ssem=DMA((2, 9 * Z)), hsem=DMA((4,)), tsem=DMA((6,)), osem=DMA((1,)), vsem=DMA((5,)), fsem=DMA((2, 5)),
+              r_sib=DMA((2, n // 2)), s_sib=DMA((2, n // 2)), r_second=DMA((2, 2 * Z)), s_second=DMA((2, 2 * Z)), r_first=DMA((2, Z)), s_first=DMA((2, Z)),
+              r_above=DMA((2, Z)), r_below=DMA((2, Z)), s_line=DMA((2, Z)))
+    res = pl.pallas_call(
+        functools.partial(fused_kernel, geo, rows, list(ins), list(outs), list(sc)),
+        out_shape=[s for _, s in outs.values()],
+        in_specs=[V] * len(ins),
+        out_specs=[b for b, _ in outs.values()],
+        scratch_shapes=list(sc.values()),
+        compiler_params=pltpu.CompilerParams(collective_id=0, has_side_effects=True, vmem_limit_bytes=64 << 20),
+        name="layer",
+    )(*ins.values())
+    mol, cg, outl, outc = res[:4]
+    return (mol.reshape(micro, span // RATE, D), cg.reshape(micro, span, D), outl.reshape(-1)[:local_params.shape[0]], outc.reshape(-1)[:conv_params.shape[0]])
+
+
+def on_device(characters, segment_ids, cotangent, local_params, conv_params):
+    n = lax.axis_size("fsdp")
+    rows = characters.shape[0] * characters.shape[1]
+    whole = n % 8 == 0 and (2 * 72 * D) % (n * UNIT) == 0 and (2 * 24 * D) % (n * UNIT) == 0
+    exact = local_params.shape[0] * n == LOCAL_COUNT and conv_params.shape[0] * n == CONV_COUNT
+    if whole and exact and rows == 4 * WINDOW:
+        return fused(n, characters, segment_ids, cotangent, local_params, conv_params)
+    return plain_device(characters, segment_ids, cotangent, local_params, conv_params)
+
+
 def solution(mesh):
     return jax.shard_map(
         on_device,
         mesh=mesh,
-        in_specs=(
-            P(None, "fsdp", None),
-            P(None, "fsdp"),
-            P(None, "fsdp", None),
-            P("fsdp"),
-            P("fsdp"),
-        ),
+        in_specs=(P(None, "fsdp", None), P(None, "fsdp"), P(None, "fsdp", None), P("fsdp"), P("fsdp")),
         out_specs=(P(None, "fsdp", None), P(None, "fsdp", None), P("fsdp"), P("fsdp")),
         check_vma=False,
     )

time: 1410 us -> 424 us (0.30)
  waiting for transfers between devices: 855 us -> 0 us
  Pallas kernels: 0 us -> 406 us
  local copies, waits for them, and re-layouts: 321 us -> 13.6 us
  matrix products: 143 us -> 0 us
  other arithmetic: 59.6 us -> 0.61 us
  between operations: 15.5 us -> 0.66 us
    unnamed x4 -> x0, waiting for transfers between devices: 855 us -> none
    pallas_call x0 -> x1, Pallas kernels: none -> 406 us  [fused(): pl.pallas_call(functools.partial(fused_kernel, geo, rows, list(ins), list...]
    dot_general x42 -> x0, matrix products: 143 us -> none  [the longest x10 52.9 us: product(): return jnp.dot(left, right, preferred_element_type=jnp.float32)]
    unnamed x256 -> x8, local copies, waits for them, and re-layouts: 109 us -> 3.37 us
    reshape x18 -> x3, local copies, waits for them, and re-layouts: 94.4 us -> 4.67 us  [the longest x1 1.81 us: fused(): jnp.pad(local_params, (0, geo.XL * LANE - local_params.shape[0]))]
    add x2 -> x0, local copies, waits for them, and re-layouts: 51 us -> none  [the longest x1 38.1 us: on_device(): local_total = local_total + local_part]
    slice x18 -> x4, local copies, waits for them, and re-layouts: 55.4 us -> 5.54 us  [the longest x1 2.14 us: fused(): outl.reshape(-1)[:local_params.shape[0]]]
    add x4 -> x0, other arithmetic: 45.1 us -> none  [the longest x1 28.6 us: on_device(): local_total = local_total + local_part]
  transfers between devices with their start and end apart: 2 -> 0, of which waited for: 2 -> 0; matrix products, arithmetic and copies ran while one was open for 0% -> 0% of each run, Pallas kernels for 0% -> 0%
where the time goes in v1:
time: 424 us; the launch traced here: 420 us
  Pallas kernels  406 us (96%)
  local copies, waits for them, and re-layouts  13.6 us (3%)
    pallas_call x1, Pallas kernels, fused(): pl.pallas_call(functools.partial(fused_kernel, geo, rows, list(ins), list...  406 us

profile of v1, /device:TPU:15, one launch (start us, length us, event | category | flops | bytes accessed | tf_op | source)
XLA Modules:
  0.0 420.4 jit_solution(3418648432831382704)
XLA Ops:
  0.6 0.7 copy.10
  1.3 1.3 reshape.43.refs_2_
  2.6 0.8 slice.13
  3.4 0.8 slice.12
  4.2 0.6 maximum_bitcast_fusion.refs_6_
  4.8 1.6 pad_bitcast_fusion.1.refs_5_
  6.4 0.9 copy.11
  7.2 1.8 pad_bitcast_fusion.refs_4_
  9.0 405.5 %layer.1 = (bf16[128,768]{1,0:T(8,128)(2,1)}, f32[512,768]{1,0:T(8,128)}, f32[1744,128]{1,0:T(8,128)}, f32[592,128]{1,0:T(8,128)}, bf16[27648,128]{1,0:T(8,128)(...) custom-call(bf16[512,768]{1,0:T(8,128)(2,1)} %bitcast.19, ...), custom_call_target="tpu_custom_call" | custom-call | tf_op jit(solution)/shard_map/layer/pallas_call | solution.py:961
  414.6 0.0 copy-start.1
  414.6 0.0 copy-start
  414.6 1.8 slice.17
  416.4 2.1 slice.16
  418.5 0.0 copy-done.1
  418.5 0.7 copy.14
  419.2 0.0 copy-done
  419.2 1.1 copy.15
Async XLA Ops:
  414.6 4.0 copy-start.1
  414.6 4.7 %copy-start = (f32[512,768]{1,0:T(8,128)S(1)}, f32[512,768]{1,0:T(8,128)}, u32[]{:S(2)}) copy-start(f32[512,768]{1,0:T(8,128)} %get-tuple-element.9) | copy-start | bytes 4718596
